TPU v7x, 512 devices: a whole 4x8x8 slice. The times are simulated.
512 devices in a mesh: dp: 8 (over z), expert: 64 (over y, x, core).
Axes of the slice: x: 4, y: 8, z: 8, core: 2. Of those that a mesh axis runs over, the one named last changes fastest.
Arguments:
- tokens: bfloat16 [65536, 3584], P(('dp', 'expert')), may hold values from -6 to 6
- cotangent: bfloat16 [65536, 3584], P(('dp', 'expert')), may hold values from -6 to 6
- route_ids: int32 [65536, 8], P(('dp', 'expert')), may hold values from 0 to 255, as said below
- route_gates: float32 [65536, 8], P(('dp', 'expert')), may hold values from 0.1 to 1
- gate_w: bfloat16 [3584, 8192], P('dp', 'expert'), may hold values from -0.09375 to 0.09375
- up_w: bfloat16 [3584, 8192], P('dp', 'expert'), may hold values from -0.09375 to 0.09375
- down_w: bfloat16 [3584, 8192], P('dp', 'expert'), may hold values from -0.1875 to 0.1875
Outputs:
- moe_out: bfloat16 [65536, 3584], P(('dp', 'expert'))
- d_tokens: bfloat16 [65536, 3584], P(('dp', 'expert'))
- d_gates: float32 [65536, 8], P(('dp', 'expert'))
- d_gate_w: bfloat16 [3584, 8192], P('dp', 'expert')
- d_up_w: bfloat16 [3584, 8192], P('dp', 'expert')
- d_down_w: bfloat16 [3584, 8192], P('dp', 'expert')
Inputs may be any that keep to these rules, and one draw needn't show every extreme that they name: `route_ids`: each token names 8 different experts; the experts in flight are 0 to 7. Among the tokens of one device (aligned blocks of 128 tokens) each expert in flight is named by at most 6 tokens, and in every draw one expert in flight is named by exactly 6 tokens in every block.
All inputs are finite; a program needn't handle non-finite values.
Results may differ from a plain program's by a relative error of at most 0.017.
Values may be sent and summed in bfloat16 or wider, within the bound.
A program may use at most 64 MiB of HBM per device.

v0:
```python
import jax
import jax.numpy as jnp
from jax import lax
from jax.sharding import Mesh, PartitionSpec as P

SLICES = 8
CAP = 6
PAD = 8
BF = jnp.bfloat16
F32 = jnp.float32
CONTRACT_COLS = (((1,), (1,)), ((), ()))
CONTRACT_ROWS = (((0,), (0,)), ((), ()))


def dot(a, b, dims=(((1,), (0,)), ((), ()))):
    return lax.dot_general(a, b, dims, preferred_element_type=F32)


def routing(route_ids, route_gates, groups):
    tok_rows = route_ids.shape[0]
    experts = jnp.arange(groups, dtype=jnp.int32)
    match = route_ids[:, :, None] == experts[None, None, :]
    member = jnp.sum(match.astype(F32), axis=1)
    gate = jnp.sum(jnp.where(match, route_gates[:, :, None], 0.0), axis=1)
    row = lax.broadcasted_iota(jnp.int32, (tok_rows, tok_rows), 0)
    col = lax.broadcasted_iota(jnp.int32, (tok_rows, tok_rows), 1)
    before = (col < row).astype(BF)
    slot = dot(before, member.astype(BF))
    return (match, member, gate, slot)


def shards(tokens, cotangent, route_ids, route_gates, gate_w, up_w, down_w):
    groups = lax.axis_size("y")
    width = tokens.shape[1]
    tok_rows = tokens.shape[0]
    hid = gate_w.shape[1]
    match, member, gate, slot = routing(route_ids, route_gates, groups)
    wide = jnp.where(member > 0.5, slot, -1.0).T[:, None, :]
    sel = (wide == jnp.arange(PAD, dtype=F32)[None, :, None]).astype(F32)
    gates_t = gate.T[:, None, :]
    slot_gate = jnp.sum(sel * gates_t, axis=2)
    pick = sel.reshape(groups * PAD, tok_rows).astype(BF)
    token_slots = dot(pick, tokens).astype(BF)
    cot_slots = dot(pick, cotangent)
    scaled_slots = (slot_gate.reshape(groups * PAD, 1) * cot_slots).astype(BF)
    send = jnp.concatenate(
        [token_slots.reshape(groups, PAD, width), scaled_slots.reshape(groups, PAD, width)], axis=1
    )
    w_all = lax.all_gather(
        jnp.concatenate([gate_w, up_w, down_w], axis=1), "dp", axis=0, tiled=True
    )
    w_gate, w_up, w_down = (w_all[:, :hid], w_all[:, hid : 2 * hid], w_all[:, 2 * hid :])
    came = lax.all_to_all(send, "y", split_axis=0, concat_axis=0, tiled=True)
    rows = groups * CAP
    out_row = lax.broadcasted_iota(jnp.int32, (2 * rows, groups * 2 * PAD), 0)
    in_row = lax.broadcasted_iota(jnp.int32, (2 * rows, groups * 2 * PAD), 1)
    kind = (out_row >= rows).astype(jnp.int32)
    local = out_row - kind * rows
    wanted = local // CAP * (2 * PAD) + kind * PAD + local % CAP
    squeeze = (in_row == wanted).astype(BF)
    compact = dot(squeeze, came.reshape(groups * 2 * PAD, width)).astype(BF)
    both = lax.all_gather(compact, ("x", "c"), axis=0, tiled=False)
    n_slices = both.shape[0]
    token_rows = both[:, :rows].reshape(n_slices * rows, width)
    scaled_rows = both[:, rows:].reshape(n_slices * rows, width)
    gate_pre = dot(token_rows, w_gate)
    up_pre = dot(token_rows, w_up)
    sig = jax.nn.sigmoid(gate_pre)
    active = gate_pre * sig
    hidden = (active * up_pre).astype(BF)
    d_hidden = dot(scaled_rows, w_down)
    d_gate_pre = (d_hidden * up_pre * sig * (1.0 + gate_pre * (1.0 - sig))).astype(BF)
    d_up_pre = (d_hidden * active).astype(BF)
    out_part = dot(hidden, w_down, CONTRACT_COLS).astype(BF)
    dx_part = (dot(d_gate_pre, w_gate, CONTRACT_COLS) + dot(d_up_pre, w_up, CONTRACT_COLS)).astype(
        BF
    )
    parts = jnp.concatenate(
        [out_part.reshape(n_slices, rows, width), dx_part.reshape(n_slices, rows, width)], axis=1
    ).reshape(n_slices * 2 * rows, width)
    summed = lax.psum_scatter(parts, ("x", "c"), scatter_dimension=0, tiled=True)
    grads = jnp.concatenate(
        [
            dot(token_rows, d_gate_pre, CONTRACT_ROWS),
            dot(token_rows, d_up_pre, CONTRACT_ROWS),
            dot(scaled_rows, hidden, CONTRACT_ROWS),
        ],
        axis=1,
    ).astype(BF)
    grads = lax.psum_scatter(grads, "dp", scatter_dimension=0, tiled=True)
    back = dot(squeeze, summed, CONTRACT_ROWS).astype(BF).reshape(groups, 2 * PAD, width)
    back = lax.all_to_all(back, "y", split_axis=0, concat_axis=0, tiled=True)
    back = back.reshape(groups * 2 * PAD, width)
    zero = jnp.zeros_like(sel)
    member_out = jnp.concatenate([sel, zero], axis=1).reshape(groups * 2 * PAD, tok_rows)
    member_dx = jnp.concatenate([zero, sel], axis=1).reshape(groups * 2 * PAD, tok_rows)
    weight = jnp.concatenate([sel * gates_t, zero], axis=1).reshape(groups * 2 * PAD, tok_rows)
    high = weight.astype(BF)
    low = (weight - high.astype(F32)).astype(BF)
    moe_out = (dot(high, back, CONTRACT_ROWS) + dot(low, back, CONTRACT_ROWS)).astype(BF)
    d_tokens = dot(member_dx.astype(BF), back, CONTRACT_ROWS).astype(BF)
    inner = dot(back, cotangent, CONTRACT_COLS) * member_out
    by_expert = jnp.sum(inner.reshape(groups, 2 * PAD, tok_rows), axis=1).T
    d_gates = jnp.sum(jnp.where(match, by_expert[:, None, :], 0.0), axis=2)
    return (
        moe_out,
        d_tokens,
        d_gates,
        grads[:, :hid],
        grads[:, hid : 2 * hid],
        grads[:, 2 * hid :],
    )


def solution(mesh):
    dp, owners = mesh.devices.shape
    y = owners // SLICES
    grid = Mesh(mesh.devices.reshape(dp, y, SLICES // 2, 2), ("dp", "y", "x", "c"))
    rows = P(("dp", "y", "x", "c"), None)
    cols = P("dp", ("y", "x", "c"))
    return jax.shard_map(
        shards,
        mesh=grid,
        in_specs=(rows, rows, rows, rows, cols, cols, cols),
        out_specs=(rows, rows, rows, cols, cols, cols),
        check_vma=False,
    )
```

profile of v0, /device:TPU:2, one launch (start us, length us, event | category | flops | bytes accessed | tf_op | source)
XLA Modules:
  0.0 255.6 jit_solution(2671036714309216586)
XLA Ops:
  7.2 0.8 convert_reduce_fusion
  8.4 1.5 fusion.6
  10.3 1.0 pad_maximum_fusion.2
  11.3 7.1 %all-to-all-start = ((bf16[8,16,3584]{2,1,0:T(8,128)(2,1)}), bf16[8,16,3584]{2,1,0:T(8,128)(2,1)S(1)}, u32[]{:S(2)}, u32[]{:S(2)}) async-start(bf16[8,16,3584]{2,1,0:T(8,128)(2,1)} %pad_maximum_fusion.2), calls=%async_computation | async-start | bytes 1835008 | tf_op jit(solution)/shard_map/all_to_all | solution.py:53
  18.5 25.8 %all-to-all-done = bf16[8,16,3584]{2,1,0:T(8,128)(2,1)S(1)} async-done(((bf16[8,16,3584]{2,1,0:T(8,128)(2,1)}), bf16[8,16,3584]{2,1,0:T(8,128)(2,1)S(1)}, u32[]{:S(2)}, u32[]{:S(2)}) %all-to-all-start) | async-done | bytes 917536 | tf_op jit(solution)/shard_map/all_to_all | solution.py:53
  44.3 1.3 convolution_convert_fusion.5
  45.7 0.8 pad_maximum_fusion.3
  46.5 40.6 %all-gather.6.cloned.1.call-done = bf16[768,3584]{1,0:T(8,128)(2,1)} async-done(((bf16[96,3584]{1,0:T(8,128)(2,1)}), bf16[768,3584]{1,0:T(8,128)(2,1)}) %all-gather.6.cloned.1.call-update) | async-done | bytes 5505040 | tf_op jit(solution)/shard_map/all_gather | solution.py:62
  87.2 5.5 %fusion.33 = (bf16[8,48,3584]{2,1,0:T(8,128)(2,1)}, bf16[8,48,3584]{2,1,0:T(8,128)(2,1)}) fusion(bf16[8,96,3584]{2,1,0:T(8,128)(2,1)} %bitcast.70), kind=kLoop, calls=%fused_computation.75 | loop fusion | bytes 11010048 | tf_op jit(solution)/shard_map/slice | solution.py:65
  92.6 44.5 %all-gather.4.cloned.1.call-done = bf16[3584,384]{1,0:T(8,128)(2,1)} async-done(((bf16[448,384]{1,0:T(8,128)(2,1)}), bf16[3584,384]{1,0:T(8,128)(2,1)}) %all-gather.4.cloned.1.call-update) | async-done | bytes 2752528 | tf_op jit(solution)/shard_map/all_gather | solution.py:49
  137.1 3.0 %fusion.15 = f32[384,128]{1,0:T(8,128)S(1)} fusion(bf16[384,3584]{1,0:T(8,128)(2,1)} %bitcast.60, bf16[3584,384]{1,0:T(8,128)(2,1)} %all-gather.4.cloned.1.call-done), kind=kOutput, calls=%fused_computation.32 | convolution fusion | flops 352321536 | bytes 3866624 | tf_op jit(solution)/shard_map/dot_general | solution.py:16
  140.2 2.2 fusion.7
  142.4 0.9 multiply_convert_fusion.2
  143.3 0.9 fusion.13
  144.2 0.9 convolution_convert_fusion
  145.0 0.9 fusion
  145.9 2.8 %pad_maximum_fusion = bf16[8,96,3584]{2,1,0:T(8,128)(2,1)} fusion(bf16[8,48,3584]{2,1,0:T(8,128)(2,1)S(1)} %bitcast.69, bf16[8,48,3584]{2,1,0:T(8,128)(2,1)S(1)} %bitcast.68), kind=kLoop, calls=%fused_computation.3 | loop fusion | flops 11010048 | bytes 11010048 | tf_op jit(solution)/shard_map/concatenate | solution.py:78
  148.8 2.6 %convolution_convert_fusion.1 = bf16[3584,128]{0,1:T(8,128)(2,1)S(1)} fusion(bf16[384,3584]{1,0:T(8,128)(2,1)} %bitcast.66, bf16[384,128]{1,0:T(8,128)(2,1)S(1)} %get-tuple-element.28), kind=kOutput, calls=%fused_computation.10 | convolution fusion | flops 352780288 | bytes 3768320 | tf_op jit(solution)/shard_map/dot_general | solution.py:16
  151.4 0.7 convolution_convert_fusion.2
  152.1 0.7 convolution_convert_fusion.3
  152.8 1.8 pad_maximum_fusion.1
  154.6 4.5 %copy.27 = bf16[3584,384]{1,0:T(8,128)(2,1)} copy(bf16[3584,384]{0,1:T(8,128)(2,1)} %pad_maximum_fusion.1) | data formatting | bytes 5505024
  159.2 30.2 %reduce-scatter.5.cloned.1.call-done = bf16[96,3584]{1,0:T(8,128)(2,1)} async-done(((bf16[768,3584]{1,0:T(8,128)(2,1)}), bf16[96,3584]{1,0:T(8,128)(2,1)}) %reduce-scatter.5.cloned.1.call-update) | async-done | bytes 688144 | tf_op jit(solution)/shard_map/reduce_scatter | solution.py:81
  189.3 2.6 %convolution_convert_fusion.4 = bf16[128,3584]{1,0:T(8,128)(2,1)} fusion(bf16[96,3584]{1,0:T(8,128)(2,1)} %reduce-scatter.5.cloned.1.call-done, s32[96]{0:T(128)S(1)} %broadcast_remainder_fusion, s32[96]{0:T(128)S(1)} %get-tuple-element.42, s32[96]{0:T(128)S(1)} %get-tuple-element.40, s32[96]{0:T(128)S(1)} %get-tuple-element.43, ...), kind=kOutput, calls=%fused_computation.13 | convolution fusion | flops 88612864 | bytes 1607744 | tf_op jit(solution)/shard_map/dot_general | solution.py:16
  191.9 6.8 %all-to-all-start.1 = ((bf16[8,16,3584]{2,1,0:T(8,128)(2,1)}), bf16[8,16,3584]{2,1,0:T(8,128)(2,1)S(1)}, u32[]{:S(2)}, u32[]{:S(2)}) async-start(bf16[8,16,3584]{2,1,0:T(8,128)(2,1)} %bitcast.12), calls=%async_computation.2 | async-start | bytes 1835008 | tf_op jit(solution)/shard_map/all_to_all | solution.py:92
  198.8 44.4 %reduce-scatter.7.cloned.1.call-done = bf16[448,384]{1,0:T(8,128)(2,1)} async-done(((bf16[3584,384]{1,0:T(8,128)(2,1)}), bf16[448,384]{1,0:T(8,128)(2,1)}) %reduce-scatter.7.cloned.1.call-update) | async-done | bytes 344080
  243.2 1.7 fusion.34
  245.0 0.4 bitcast_reduce_fusion
  245.4 0.6 select_reduce_fusion
  246.0 0.4 convolution_bitcast_fusion.1
  246.4 1.4 fusion.2
  247.8 1.3 fusion.3
  (39 shorter events, 1.1 us)
Async XLA Ops:
  7.2 2.8 %copy-start = (bf16[128,3584]{1,0:T(8,128)(2,1)S(1)}, bf16[128,3584]{1,0:T(8,128)(2,1)}, u32[]{:S(2)}) copy-start(bf16[128,3584]{1,0:T(8,128)(2,1)} %param.8) | copy-start | bytes 2752516
  10.3 35.4 %copy-start.5 = (bf16[448,128]{1,0:T(8,128)(2,1)S(1)}, bf16[448,128]{1,0:T(8,128)(2,1)}, u32[]{:S(2)}) copy-start(bf16[448,128]{1,0:T(8,128)(2,1)} %param.13) | copy-start | bytes 344068
  10.3 35.4 %copy-start.6 = (bf16[448,128]{1,0:T(8,128)(2,1)S(1)}, bf16[448,128]{1,0:T(8,128)(2,1)}, u32[]{:S(2)}) copy-start(bf16[448,128]{1,0:T(8,128)(2,1)} %param.12) | copy-start | bytes 344068
  10.3 35.4 %copy-start.7 = (bf16[448,128]{1,0:T(8,128)(2,1)S(1)}, bf16[448,128]{1,0:T(8,128)(2,1)}, u32[]{:S(2)}) copy-start(bf16[448,128]{1,0:T(8,128)(2,1)} %param.11) | copy-start | bytes 344068
  11.3 33.0 %all-to-all-start = ((bf16[8,16,3584]{2,1,0:T(8,128)(2,1)}), bf16[8,16,3584]{2,1,0:T(8,128)(2,1)S(1)}, u32[]{:S(2)}, u32[]{:S(2)}) async-start(bf16[8,16,3584]{2,1,0:T(8,128)(2,1)} %pad_maximum_fusion.2), calls=%async_computation | async-start | bytes 1835008 | tf_op jit(solution)/shard_map/all_to_all | solution.py:53
  18.4 68.8 %all-gather.6.cloned.1.call-start = ((), (), s32[]{:S(2)}) async-start(), calls=%async_computation.6 | async-start | bytes 6193152 | tf_op jit(solution)/shard_map/all_gather | solution.py:62
  45.6 91.5 %all-gather.4.cloned.1.call-start = ((), (), s32[]{:S(2)}) async-start(), calls=%async_computation.4 | async-start | bytes 3096576 | tf_op jit(solution)/shard_map/all_gather | solution.py:49
  46.5 142.8 %reduce-scatter.5.cloned.1.call-start = ((), (), s32[]{:S(2)}) async-start(), calls=%async_computation.5 | async-start | bytes 6193152 | tf_op jit(solution)/shard_map/reduce_scatter | solution.py:81
  137.1 3.0 %copy-start.3 = (bf16[8,48,3584]{2,1,0:T(8,128)(2,1)S(1)}, bf16[8,48,3584]{2,1,0:T(8,128)(2,1)}, u32[]{:S(2)}) copy-start(bf16[8,48,3584]{2,1,0:T(8,128)(2,1)} %get-tuple-element.26) | copy-start | bytes 8257540
  137.1 5.3 %copy-start.4 = (bf16[3584,384]{1,0:T(8,128)(2,1)S(1)}, bf16[3584,384]{1,0:T(8,128)(2,1)}, u32[]{:S(2)}) copy-start(bf16[3584,384]{1,0:T(8,128)(2,1)} %all-gather.4.cloned.1.call-done) | copy-start | bytes 8257540
  140.2 2.2 copy-start.1
  148.7 94.5 %reduce-scatter.7.cloned.1.call-start = ((), (), s32[]{:S(2)}) async-start(), calls=%async_computation.7 | async-start | bytes 3096576
  148.8 2.6 %copy-start.2 = (bf16[8,48,3584]{2,1,0:T(8,128)(2,1)S(1)}, bf16[8,48,3584]{2,1,0:T(8,128)(2,1)}, u32[]{:S(2)}) copy-start(bf16[8,48,3584]{2,1,0:T(8,128)(2,1)} %get-tuple-element.27) | copy-start | bytes 8257540
  159.2 86.2 %copy-start.8 = (s32[128,8]{0,1:T(8,128)S(1)}, s32[128,8]{0,1:T(8,128)}, u32[]{:S(2)}) copy-start(s32[128,8]{0,1:T(8,128)} %param.9) | copy-start | bytes 12292
  191.9 53.0 %all-to-all-start.1 = ((bf16[8,16,3584]{2,1,0:T(8,128)(2,1)}), bf16[8,16,3584]{2,1,0:T(8,128)(2,1)S(1)}, u32[]{:S(2)}, u32[]{:S(2)}) async-start(bf16[8,16,3584]{2,1,0:T(8,128)(2,1)} %bitcast.12), calls=%async_computation.2 | async-start | bytes 1835008 | tf_op jit(solution)/shard_map/all_to_all | solution.py:92
Sparse Core Ops, SparseCore 0:
  45.7 41.3 all-gather.5
  89.8 47.2 all-gather.3
  148.8 40.4 reduce-scatter.4
  192.0 51.1 reduce-scatter.6
where the time goes:
time: 256 us
  waiting for transfers between devices  186 us (73%)
  matrix products  22.1 us (9%)
  starting transfers between devices  14.1 us (6%)
  between operations  14 us (5%)
  local copies, waits for them, and re-layouts  12 us (5%)
  other arithmetic  7.87 us (3%)
    unnamed x5, waiting for transfers between devices  44.5 us
    all_gather x1, waiting for transfers between devices, shards(): lax.all_gather(jnp.concatenate([gate_w, up_w, down_w], axis=1), 'dp', axi...  44.5 us
    all_gather x1, waiting for transfers between devices, shards(): both = lax.all_gather(compact, ('x', 'c'), axis=0, tiled=False)  40.6 us
    reduce_scatter x1, waiting for transfers between devices, shards(): lax.psum_scatter(parts, ('x', 'c'), scatter_dimension=0, tiled=True)  30.2 us
    all_to_all x1, waiting for transfers between devices, shards(): came = lax.all_to_all(send, 'y', split_axis=0, concat_axis=0, tiled=True)  25.8 us
    dot_general x18, matrix products, dot(): return lax.dot_general(a, b, dims, preferred_element_type=F32)  22.1 us
    all_to_all x1, starting transfers between devices, shards(): came = lax.all_to_all(send, 'y', split_axis=0, concat_axis=0, tiled=True)  7.09 us
    all_to_all x1, starting transfers between devices, shards(): back = lax.all_to_all(back, 'y', split_axis=0, concat_axis=0, tiled=True)  6.82 us
  transfers between devices with their start and end apart: 6, of which 5 were waited for; matrix products, arithmetic and copies ran while one was open for 8% of the time, Pallas kernels for 0%

commit v1 on v0

--- a/solution.py
+++ b/solution.py
@@ -10,6 +10,13 @@
 F32 = jnp.float32
 CONTRACT_COLS = (((1,), (1,)), ((), ()))
 CONTRACT_ROWS = (((0,), (0,)), ((), ()))
+
+
+def swapped_in(value, mesh_axis, dim):
+    count = lax.axis_size(mesh_axis)
+    blocks = jnp.stack([value for _ in range(count)])
+    blocks = lax.all_to_all(blocks, mesh_axis, split_axis=0, concat_axis=0)
+    return jnp.concatenate(blocks, axis=dim)
 
 
 def dot(a, b, dims=(((1,), (0,)), ((), ()))):
@@ -46,9 +53,7 @@
     send = jnp.concatenate(
         [token_slots.reshape(groups, PAD, width), scaled_slots.reshape(groups, PAD, width)], axis=1
     )
-    w_all = lax.all_gather(
-        jnp.concatenate([gate_w, up_w, down_w], axis=1), "dp", axis=0, tiled=True
-    )
+    w_all = swapped_in(jnp.concatenate([gate_w, up_w, down_w], axis=1), "dp", 0)
     w_gate, w_up, w_down = (w_all[:, :hid], w_all[:, hid : 2 * hid], w_all[:, 2 * hid :])
     came = lax.all_to_all(send, "y", split_axis=0, concat_axis=0, tiled=True)
     rows = groups * CAP

time: 256 us -> 241 us (0.941)
  waiting for transfers between devices: 186 us -> 154 us
  starting transfers between devices: 14.1 us -> 24.4 us
  matrix products: 22.1 us -> 26.9 us
    all_gather x1 -> x0, waiting for transfers between devices: 44.5 us -> none  [shards(): lax.all_gather(jnp.concatenate([gate_w, up_w, down_w], axis=1), 'dp', axi...]
    all_to_all x0 -> x1, waiting for transfers between devices: none -> 30.7 us  [swapped_in(): blocks = lax.all_to_all(blocks, mesh_axis, split_axis=0, concat_axis=0)]
    all_gather x1, waiting for transfers between devices: 40.6 us -> 29.3 us  [shards(): both = lax.all_gather(compact, ('x', 'c'), axis=0, tiled=False)]
    all_to_all x0 -> x1, starting transfers between devices: none -> 10.3 us  [swapped_in(): blocks = lax.all_to_all(blocks, mesh_axis, split_axis=0, concat_axis=0)]
    reduce_scatter x1, waiting for transfers between devices: 30.2 us -> 22.9 us  [shards(): lax.psum_scatter(parts, ('x', 'c'), scatter_dimension=0, tiled=True)]
    dot_general x18, matrix products: 22.1 us -> 26.9 us  [dot(): return lax.dot_general(a, b, dims, preferred_element_type=F32)]
    unnamed x5 -> x4, waiting for transfers between devices: 44.5 us -> 44.9 us
  transfers between devices with their start and end apart: 6 -> 6, of which waited for: 5 -> 5; matrix products, arithmetic and copies ran while one was open for 8% -> 9% of each run, Pallas kernels for 0% -> 0%
where the time goes in v1:
time: 241 us; the launch traced here: 240 us
  waiting for transfers between devices  154 us (64%)
  matrix products  26.9 us (11%)
  starting transfers between devices  24.4 us (10%)
  between operations  14 us (6%)
  local copies, waits for them, and re-layouts  13.8 us (6%)
  other arithmetic  7.16 us (3%)
    unnamed x4, waiting for transfers between devices  44.9 us
    all_to_all x1, waiting for transfers between devices, swapped_in(): blocks = lax.all_to_all(blocks, mesh_axis, split_axis=0, concat_axis=0)  30.7 us
    all_gather x1, waiting for transfers between devices, shards(): both = lax.all_gather(compact, ('x', 'c'), axis=0, tiled=False)  29.3 us
    dot_general x18, matrix products, dot(): return lax.dot_general(a, b, dims, preferred_element_type=F32)  26.9 us
    all_to_all x1, waiting for transfers between devices, shards(): came = lax.all_to_all(send, 'y', split_axis=0, concat_axis=0, tiled=True)  25.8 us
    reduce_scatter x1, waiting for transfers between devices, shards(): lax.psum_scatter(parts, ('x', 'c'), scatter_dimension=0, tiled=True)  22.9 us
    all_to_all x1, starting transfers between devices, swapped_in(): blocks = lax.all_to_all(blocks, mesh_axis, split_axis=0, concat_axis=0)  10.3 us
    all_to_all x1, starting transfers between devices, shards(): came = lax.all_to_all(send, 'y', split_axis=0, concat_axis=0, tiled=True)  7.09 us
  transfers between devices with their start and end apart: 6, of which 5 were waited for; matrix products, arithmetic and copies ran while one was open for 9% of the time, Pallas kernels for 0%

profile of v1, /device:TPU:2, one launch (start us, length us, event | category | flops | bytes accessed | tf_op | source)
XLA Modules:
  0.0 239.8 jit_solution(6471828938322069583)
XLA Ops:
  7.2 0.8 convert_reduce_fusion
  8.4 1.5 fusion.6
  10.3 1.0 pad_maximum_fusion.2
  11.3 7.1 %all-to-all-start = ((bf16[8,16,3584]{2,1,0:T(8,128)(2,1)}), bf16[8,16,3584]{2,1,0:T(8,128)(2,1)S(1)}, u32[]{:S(2)}, u32[]{:S(2)}) async-start(bf16[8,16,3584]{2,1,0:T(8,128)(2,1)} %pad_maximum_fusion.2), calls=%async_computation | async-start | bytes 1835008 | tf_op jit(solution)/shard_map/all_to_all | solution.py:58
  18.5 25.8 %all-to-all-done = bf16[8,16,3584]{2,1,0:T(8,128)(2,1)S(1)} async-done(((bf16[8,16,3584]{2,1,0:T(8,128)(2,1)}), bf16[8,16,3584]{2,1,0:T(8,128)(2,1)S(1)}, u32[]{:S(2)}, u32[]{:S(2)}) %all-to-all-start) | async-done | bytes 917536 | tf_op jit(solution)/shard_map/all_to_all | solution.py:58
  44.3 1.3 convolution_convert_fusion.5
  45.7 1.8 stack.2
  47.5 10.3 %all-to-all-start.1 = ((bf16[8,448,384]{2,1,0:T(8,128)(2,1)}), bf16[8,448,384]{2,1,0:T(8,128)(2,1)}, u32[]{:S(2)}, u32[]{:S(2)}) async-start(bf16[8,448,384]{2,1,0:T(8,128)(2,1)} %stack.2), calls=%async_computation.1 | async-start | bytes 5505024 | tf_op jit(solution)/shard_map/all_to_all | solution.py:18
  57.8 29.3 %all-gather.3.cloned.1.call-done = bf16[768,3584]{1,0:T(8,128)(2,1)} async-done(((bf16[96,3584]{1,0:T(8,128)(2,1)}), bf16[768,3584]{1,0:T(8,128)(2,1)}) %all-gather.3.cloned.1.call-update) | async-done | bytes 5505040 | tf_op jit(solution)/shard_map/all_gather | solution.py:67
  87.2 5.5 %fusion.33 = (bf16[8,48,3584]{2,1,0:T(8,128)(2,1)}, bf16[8,48,3584]{2,1,0:T(8,128)(2,1)}) fusion(bf16[8,96,3584]{2,1,0:T(8,128)(2,1)} %bitcast.71), kind=kLoop, calls=%fused_computation.75 | loop fusion | bytes 11010048 | tf_op jit(solution)/shard_map/slice | solution.py:70
  92.6 30.7 %all-to-all-done.1 = bf16[8,448,384]{2,1,0:T(8,128)(2,1)} async-done(((bf16[8,448,384]{2,1,0:T(8,128)(2,1)}), bf16[8,448,384]{2,1,0:T(8,128)(2,1)}, u32[]{:S(2)}, u32[]{:S(2)}) %all-to-all-start.1) | async-done | bytes 2752544 | tf_op jit(solution)/shard_map/all_to_all | solution.py:18
  123.4 3.0 %fusion.15 = f32[384,128]{1,0:T(8,128)S(1)} fusion(bf16[384,3584]{1,0:T(8,128)(2,1)} %bitcast.61, bf16[3584,384]{1,0:T(8,128)(2,1)} %bitcast.8), kind=kOutput, calls=%fused_computation.32 | convolution fusion | flops 352321536 | bytes 3866624 | tf_op jit(solution)/shard_map/dot_general | solution.py:23
  126.4 2.2 fusion.7
  128.6 2.1 multiply_convert_fusion.2
  130.7 2.1 fusion.13
  132.8 2.1 convolution_convert_fusion
  134.8 2.1 fusion
  136.9 2.8 %pad_maximum_fusion = bf16[8,96,3584]{2,1,0:T(8,128)(2,1)} fusion(bf16[8,48,3584]{2,1,0:T(8,128)(2,1)S(1)} %bitcast.70, bf16[8,48,3584]{2,1,0:T(8,128)(2,1)S(1)} %bitcast.69), kind=kLoop, calls=%fused_computation.3 | loop fusion | flops 11010048 | bytes 11010048 | tf_op jit(solution)/shard_map/concatenate | solution.py:83
  139.7 2.6 %convolution_convert_fusion.1 = bf16[3584,128]{0,1:T(8,128)(2,1)S(1)} fusion(bf16[384,3584]{1,0:T(8,128)(2,1)} %bitcast.67, bf16[384,128]{1,0:T(8,128)(2,1)S(1)} %get-tuple-element.28), kind=kOutput, calls=%fused_computation.10 | convolution fusion | flops 352780288 | bytes 3768320 | tf_op jit(solution)/shard_map/dot_general | solution.py:23
  142.4 0.7 convolution_convert_fusion.2
  143.1 0.7 convolution_convert_fusion.3
  143.8 1.8 pad_maximum_fusion.1
  145.6 4.6 %copy.27 = bf16[3584,384]{1,0:T(8,128)(2,1)} copy(bf16[3584,384]{0,1:T(8,128)(2,1)} %pad_maximum_fusion.1) | data formatting | bytes 5505024
  150.2 22.9 %reduce-scatter.5.cloned.1.call-done = bf16[96,3584]{1,0:T(8,128)(2,1)} async-done(((bf16[768,3584]{1,0:T(8,128)(2,1)}), bf16[96,3584]{1,0:T(8,128)(2,1)}) %reduce-scatter.5.cloned.1.call-update) | async-done | bytes 688144 | tf_op jit(solution)/shard_map/reduce_scatter | solution.py:86
  173.1 2.6 %convolution_convert_fusion.4 = bf16[128,3584]{1,0:T(8,128)(2,1)} fusion(bf16[96,3584]{1,0:T(8,128)(2,1)} %reduce-scatter.5.cloned.1.call-done, s32[96]{0:T(128)S(1)} %broadcast_remainder_fusion, s32[96]{0:T(128)S(1)} %get-tuple-element.42, s32[96]{0:T(128)S(1)} %get-tuple-element.40, s32[96]{0:T(128)S(1)} %get-tuple-element.43, ...), kind=kOutput, calls=%fused_computation.13 | convolution fusion | flops 88612864 | bytes 1607744 | tf_op jit(solution)/shard_map/dot_general | solution.py:23
  175.7 6.9 %all-to-all-start.2 = ((bf16[8,16,3584]{2,1,0:T(8,128)(2,1)}), bf16[8,16,3584]{2,1,0:T(8,128)(2,1)S(1)}, u32[]{:S(2)}, u32[]{:S(2)}) async-start(bf16[8,16,3584]{2,1,0:T(8,128)(2,1)} %bitcast.13), calls=%async_computation.3 | async-start | bytes 1835008 | tf_op jit(solution)/shard_map/all_to_all | solution.py:97
  182.6 44.8 %reduce-scatter.7.cloned.1.call-done = bf16[448,384]{1,0:T(8,128)(2,1)} async-done(((bf16[3584,384]{1,0:T(8,128)(2,1)}), bf16[448,384]{1,0:T(8,128)(2,1)}) %reduce-scatter.7.cloned.1.call-update) | async-done | bytes 344080
  227.4 1.7 fusion.34
  229.6 0.6 select_reduce_fusion
  230.2 0.4 convolution_bitcast_fusion.1
  230.6 1.4 fusion.2
  232.0 1.3 fusion.3
  (37 shorter events, 1.5 us)
Async XLA Ops:
  7.2 2.8 %copy-start = (bf16[128,3584]{1,0:T(8,128)(2,1)S(1)}, bf16[128,3584]{1,0:T(8,128)(2,1)}, u32[]{:S(2)}) copy-start(bf16[128,3584]{1,0:T(8,128)(2,1)} %param.8) | copy-start | bytes 2752516
  10.3 35.4 %copy-start.4 = (bf16[448,128]{1,0:T(8,128)(2,1)S(1)}, bf16[448,128]{1,0:T(8,128)(2,1)}, u32[]{:S(2)}) copy-start(bf16[448,128]{1,0:T(8,128)(2,1)} %param.13) | copy-start | bytes 344068
  10.3 35.4 %copy-start.5 = (bf16[448,128]{1,0:T(8,128)(2,1)S(1)}, bf16[448,128]{1,0:T(8,128)(2,1)}, u32[]{:S(2)}) copy-start(bf16[448,128]{1,0:T(8,128)(2,1)} %param.12) | copy-start | bytes 344068
  10.3 35.3 %copy-start.6 = (bf16[448,128]{1,0:T(8,128)(2,1)S(1)}, bf16[448,128]{1,0:T(8,128)(2,1)}, u32[]{:S(2)}) copy-start(bf16[448,128]{1,0:T(8,128)(2,1)} %param.11) | copy-start | bytes 344068
  11.3 33.0 %all-to-all-start = ((bf16[8,16,3584]{2,1,0:T(8,128)(2,1)}), bf16[8,16,3584]{2,1,0:T(8,128)(2,1)S(1)}, u32[]{:S(2)}, u32[]{:S(2)}) async-start(bf16[8,16,3584]{2,1,0:T(8,128)(2,1)} %pad_maximum_fusion.2), calls=%async_computation | async-start | bytes 1835008 | tf_op jit(solution)/shard_map/all_to_all | solution.py:58
  18.4 68.8 %all-gather.3.cloned.1.call-start = ((), (), s32[]{:S(2)}) async-start(), calls=%async_computation.6 | async-start | bytes 6193152 | tf_op jit(solution)/shard_map/all_gather | solution.py:67
  47.5 75.9 %all-to-all-start.1 = ((bf16[8,448,384]{2,1,0:T(8,128)(2,1)}), bf16[8,448,384]{2,1,0:T(8,128)(2,1)}, u32[]{:S(2)}, u32[]{:S(2)}) async-start(bf16[8,448,384]{2,1,0:T(8,128)(2,1)} %stack.2), calls=%async_computation.1 | async-start | bytes 5505024 | tf_op jit(solution)/shard_map/all_to_all | solution.py:18
  57.8 115.3 %reduce-scatter.5.cloned.1.call-start = ((), (), s32[]{:S(2)}) async-start(), calls=%async_computation.5 | async-start | bytes 6193152 | tf_op jit(solution)/shard_map/reduce_scatter | solution.py:86
  123.4 3.0 %copy-start.3 = (bf16[8,48,3584]{2,1,0:T(8,128)(2,1)S(1)}, bf16[8,48,3584]{2,1,0:T(8,128)(2,1)}, u32[]{:S(2)}) copy-start(bf16[8,48,3584]{2,1,0:T(8,128)(2,1)} %get-tuple-element.26) | copy-start | bytes 8257540
  126.4 2.2 copy-start.1
  139.7 87.7 %reduce-scatter.7.cloned.1.call-start = ((), (), s32[]{:S(2)}) async-start(), calls=%async_computation.7 | async-start | bytes 3096576
  139.7 2.6 %copy-start.2 = (bf16[8,48,3584]{2,1,0:T(8,128)(2,1)S(1)}, bf16[8,48,3584]{2,1,0:T(8,128)(2,1)}, u32[]{:S(2)}) copy-start(bf16[8,48,3584]{2,1,0:T(8,128)(2,1)} %get-tuple-element.27) | copy-start | bytes 8257540
  150.2 79.4 %copy-start.7 = (s32[128,8]{0,1:T(8,128)S(1)}, s32[128,8]{0,1:T(8,128)}, u32[]{:S(2)}) copy-start(s32[128,8]{0,1:T(8,128)} %param.9) | copy-start | bytes 12292
  175.7 53.5 %all-to-all-start.2 = ((bf16[8,16,3584]{2,1,0:T(8,128)(2,1)}), bf16[8,16,3584]{2,1,0:T(8,128)(2,1)S(1)}, u32[]{:S(2)}, u32[]{:S(2)}) async-start(bf16[8,16,3584]{2,1,0:T(8,128)(2,1)} %bitcast.13), calls=%async_computation.3 | async-start | bytes 1835008 | tf_op jit(solution)/shard_map/all_to_all | solution.py:97
Sparse Core Ops, SparseCore 0:
  45.7 41.3 all-gather.2
  139.8 33.2 reduce-scatter.4
  176.0 51.4 reduce-scatter.6
